TPU v7x, 128 devices: a whole 4x4x4 slice. The times are simulated.
128 devices in a mesh: row: 8 (over y, core), col: 16 (over z, x).
Axes of the slice: x: 4, y: 4, z: 4, core: 2. Of those that a mesh axis runs over, the one named last changes fastest.
Arguments:
- pair_rows: int32 [18432, 768], P(('row', 'col')), may hold values from 0 to 4095, as said below
- pair_cols: int32 [18432, 768], P(('row', 'col')), may hold values from 0 to 8191
- pair_weights: float32 [18432, 768], P(('row', 'col')), may hold values from 0.2 to 6, as said below
- block_counts: int32 [18432], P(('row', 'col')), may hold values from 576 to 768, as said below
Outputs:
- balanced: float32 [4096, 8192], P('row', 'col')
- row_bias: float32 [4096], P('row')
- col_bias: float32 [8192], P('col')
Inputs may be any that keep to these rules, and one draw needn't show every extreme that they name: `pair_rows`: all entries of one block lie in one aligned 128 x 128 square of one 512 x 512 tile of the map (tiles counted from bin 0 along both sides). Among the blocks of one device, every tile whose tile row differs from its tile column has exactly one block, and every tile whose tile row equals its tile column has exactly 3. `pair_weights`: positive weights. Only the first block_counts entries of a block are read pairs.
All inputs are finite; a program needn't handle non-finite values.
Results may differ from a plain program's by a relative error of at most 0.0001.
Values sent between devices are 32-bit elements; how exact they have to be, the bound alone decides.
No kernel may reach another device: no remote copies, remote signals or barrier semaphores. Data moves between devices by JAX's collectives and lax.ppermute only.
A program may use at most 64 MiB of HBM per device.

v0:
```python
import math

import jax
import jax.numpy as jnp
from jax import lax
from jax.sharding import PartitionSpec as P

TILE = 512
SUB = 128
SLOT = 3
SWEEPS = 2


prior_count = 0.015625
block_group = 16


def bin_blocks(positions, weights):
    count_blocks, block_cap = positions.shape
    per_side = TILE // SUB
    squares = per_side * per_side
    group = math.gcd(count_blocks, block_group)
    first = positions[:, 0]
    square_id = first // TILE // SUB * per_side + first % TILE // SUB
    local_row = (positions // TILE % SUB).reshape(count_blocks // group, group, block_cap)
    local_col = (positions % TILE % SUB).reshape(count_blocks // group, group, block_cap)
    weight_groups = weights.reshape(count_blocks // group, group, block_cap)
    square_groups = square_id.reshape(count_blocks // group, group)

    def add_group(group_idx, running):
        rows_now = local_row[group_idx]
        cols_now = local_col[group_idx]
        wgt_now = weight_groups[group_idx]
        lanes = lax.broadcasted_iota(jnp.int32, (group, block_cap, SUB), 2)
        row_hot = jnp.where(rows_now[:, :, None] == lanes, wgt_now[:, :, None], 0.0)
        col_hot = (cols_now[:, :, None] == lanes).astype(jnp.float32)
        pieces = jnp.einsum("gkr,gkc->grc", row_hot, col_hot, precision=lax.Precision.HIGHEST)
        square_lanes = lax.broadcasted_iota(jnp.int32, (group, squares), 1)
        choose = (square_groups[group_idx][:, None] == square_lanes).astype(jnp.float32)
        return running + jnp.einsum("gs,grc->src", choose, pieces, precision=lax.Precision.HIGHEST)

    running = lax.fori_loop(
        0, count_blocks // group, add_group, jnp.zeros((squares, SUB, SUB), jnp.float32)
    )
    return running.reshape(per_side, per_side, SUB, SUB).transpose(0, 2, 1, 3).reshape(TILE, TILE)


def pack_slots(positions, masked, target, slots):
    wanted = lax.broadcasted_iota(jnp.int32, (slots, target.shape[0]), 0)
    match = wanted == target[None, :]
    present = jnp.any(match, axis=1)
    chosen = jnp.argmax(match, axis=1)
    send_pos = jnp.where(present[:, None], positions[chosen], 0)
    send_wgt = jnp.where(present[:, None], masked[chosen], 0.0)
    return (send_pos, send_wgt)


def deliver_owner(send_pos, send_wgt):
    return (
        lax.all_to_all(send_pos, ("row", "col"), split_axis=0, concat_axis=0, tiled=True),
        lax.all_to_all(send_wgt, ("row", "col"), split_axis=0, concat_axis=0, tiled=True),
    )


def row_grand_total(row_sums):
    return lax.psum(jnp.sum(row_sums), "row")


def col_grand_total(col_sums):
    return lax.psum(jnp.sum(col_sums), "col")


def on_device(pair_rows, pair_cols, pair_weights, block_counts):
    n_row = lax.axis_size("row")
    n_col = lax.axis_size("col")
    devices = n_row * n_col
    count_blocks, block_cap = pair_rows.shape
    entry_pos = lax.broadcasted_iota(jnp.int32, (count_blocks, block_cap), 1)
    masked = jnp.where(entry_pos < block_counts[:, None], pair_weights, 0.0)
    positions = pair_rows % TILE * TILE + pair_cols % TILE
    tile_row = pair_rows[:, 0] // TILE
    tile_col = pair_cols[:, 0] // TILE
    owner_dev = tile_row * n_col + tile_col
    later = lax.broadcasted_iota(jnp.int32, (count_blocks, count_blocks), 0)
    sooner = lax.broadcasted_iota(jnp.int32, (count_blocks, count_blocks), 1)
    same_dest = (owner_dev[:, None] == owner_dev[None, :]) & (sooner < later)
    slot_rank = jnp.sum(same_dest.astype(jnp.int32), axis=1)
    target = owner_dev * SLOT + slot_rank
    send_pos, send_wgt = pack_slots(positions, masked, target, devices * SLOT)
    send_pos = send_pos.reshape(devices, SLOT, block_cap)
    send_wgt = send_wgt.reshape(devices, SLOT, block_cap)
    got_pos, got_wgt = deliver_owner(send_pos, send_wgt)
    tile_sum = bin_blocks(
        got_pos.reshape(devices * SLOT, block_cap), got_wgt.reshape(devices * SLOT, block_cap)
    )
    balanced = tile_sum + prior_count
    row_bias = jnp.ones((TILE,), jnp.float32)
    col_bias = jnp.ones((TILE,), jnp.float32)
    r_bins = TILE * n_row
    c_bins = TILE * n_col
    for sweep_idx in range(SWEEPS):
        row_sums = lax.psum(jnp.sum(balanced, axis=1), "col")
        row_mean = row_grand_total(row_sums) / r_bins
        ratio = row_sums / row_mean
        balanced = balanced / ratio[:, None]
        row_bias = row_bias * ratio
        col_sums = lax.psum(jnp.sum(balanced, axis=0), "row")
        col_mean = col_grand_total(col_sums) / c_bins
        factor = col_sums / col_mean
        balanced = balanced / factor[None, :]
        col_bias = col_bias * factor
    return (balanced, row_bias, col_bias)


def solution(mesh):
    return jax.shard_map(
        on_device,
        mesh=mesh,
        in_specs=(
            P(("row", "col"), None),
            P(("row", "col"), None),
            P(("row", "col"), None),
            P(("row", "col")),
        ),
        out_specs=(P("row", "col"), P("row"), P("col")),
        check_vma=False,
    )
```

profile of v0, /device:TPU:1, one launch (start us, length us, event | category | flops | bytes accessed | tf_op | source)
XLA Modules:
  0.0 525.7 jit_solution(288508678104768664)
XLA Ops:
  8.6 11.5 %all-to-all-start = ((s32[128,3,768]{2,1,0:T(4,128)}), s32[128,3,768]{2,1,0:T(4,128)S(1)}, u32[]{:S(2)}, u32[]{:S(2)}) async-start(s32[128,3,768]{2,1,0:T(4,128)} %broadcast_select_fusion.1), calls=%async_computation | async-start | bytes 3145728 | tf_op jit(solution)/shard_map/all_to_all | solution.py:60
  28.1 16.0 %all-to-all-done = s32[128,3,768]{2,1,0:T(4,128)S(1)} async-done(((s32[128,3,768]{2,1,0:T(4,128)}), s32[128,3,768]{2,1,0:T(4,128)S(1)}, u32[]{:S(2)}, u32[]{:S(2)}) %all-to-all-start) | async-done | bytes 1179680 | tf_op jit(solution)/shard_map/all_to_all | solution.py:60
  57.2 16.8 %all-to-all-done.1 = f32[128,3,768]{2,1,0:T(4,128)} async-done(((f32[128,3,768]{2,1,0:T(4,128)}), f32[128,3,768]{2,1,0:T(4,128)}, u32[]{:S(2)}, u32[]{:S(2)}) %all-to-all-start.1) | async-done | bytes 1179680 | tf_op jit(solution)/shard_map/all_to_all | solution.py:61
  76.5 239.1 %while.14 = (s32[]{:T(128)}, f32[16,128,128]{2,0,1:T(8,128)S(1)}, s32[24,16]{1,0:T(8,128)S(1)}, s32[24,16,768]{2,1,0:T(8,128)S(1)}, f32[24,16,768]{2,1,0:T(8,128...) while((s32[]{:T(128)}, f32[16,128,128]{2,0,1:T(8,128)S(1)}, s32[24,16]{1,0:T(8,128)S(1)}, ...), condition=%wide.region_4.5_spmd.clone, body=%wide.region_3.4_spmd.clone.sunk | while | flops 2471493888 | bytes 4636979 | solution.py:42
  77.3 7.5 %fusion.55 = f32[16,128,128]{2,1,0:T(8,128)S(1)} fusion(s32[16,768]{1,0:T(8,128)S(1)} %get-tuple-element.198, f32[16,768]{1,0:T(8,128)S(1)} %dynamic-slice_bitcast_fusion.6, s32[16,768]{1,0:T(8,128)S(1)} %get-tuple-element.199), kind=kOutput, calls=%fused_computation.3.clone.1 | convolution fusion | flops 2420637696 | bytes 1196032 | tf_op jit(solution)/shard_map/while/body/eval_jaxpr/gkr,gkc->grc/dot_general | solution.py:37
  87.3 7.5 %fusion.55 = f32[16,128,128]{2,1,0:T(8,128)S(1)} fusion(s32[16,768]{1,0:T(8,128)S(1)} %get-tuple-element.198, f32[16,768]{1,0:T(8,128)S(1)} %dynamic-slice_bitcast_fusion.6, s32[16,768]{1,0:T(8,128)S(1)} %get-tuple-element.199), kind=kOutput, calls=%fused_computation.3.clone.1 | convolution fusion | flops 2420637696 | bytes 1196032 | tf_op jit(solution)/shard_map/while/body/eval_jaxpr/gkr,gkc->grc/dot_general | solution.py:37
  97.2 7.5 %fusion.55 = f32[16,128,128]{2,1,0:T(8,128)S(1)} fusion(s32[16,768]{1,0:T(8,128)S(1)} %get-tuple-element.198, f32[16,768]{1,0:T(8,128)S(1)} %dynamic-slice_bitcast_fusion.6, s32[16,768]{1,0:T(8,128)S(1)} %get-tuple-element.199), kind=kOutput, calls=%fused_computation.3.clone.1 | convolution fusion | flops 2420637696 | bytes 1196032 | tf_op jit(solution)/shard_map/while/body/eval_jaxpr/gkr,gkc->grc/dot_general | solution.py:37
  107.2 7.5 %fusion.55 = f32[16,128,128]{2,1,0:T(8,128)S(1)} fusion(s32[16,768]{1,0:T(8,128)S(1)} %get-tuple-element.198, f32[16,768]{1,0:T(8,128)S(1)} %dynamic-slice_bitcast_fusion.6, s32[16,768]{1,0:T(8,128)S(1)} %get-tuple-element.199), kind=kOutput, calls=%fused_computation.3.clone.1 | convolution fusion | flops 2420637696 | bytes 1196032 | tf_op jit(solution)/shard_map/while/body/eval_jaxpr/gkr,gkc->grc/dot_general | solution.py:37
  117.2 7.5 %fusion.55 = f32[16,128,128]{2,1,0:T(8,128)S(1)} fusion(s32[16,768]{1,0:T(8,128)S(1)} %get-tuple-element.198, f32[16,768]{1,0:T(8,128)S(1)} %dynamic-slice_bitcast_fusion.6, s32[16,768]{1,0:T(8,128)S(1)} %get-tuple-element.199), kind=kOutput, calls=%fused_computation.3.clone.1 | convolution fusion | flops 2420637696 | bytes 1196032 | tf_op jit(solution)/shard_map/while/body/eval_jaxpr/gkr,gkc->grc/dot_general | solution.py:37
  137.1 7.5 %fusion.55 = f32[16,128,128]{2,1,0:T(8,128)S(1)} fusion(s32[16,768]{1,0:T(8,128)S(1)} %get-tuple-element.198, f32[16,768]{1,0:T(8,128)S(1)} %dynamic-slice_bitcast_fusion.6, s32[16,768]{1,0:T(8,128)S(1)} %get-tuple-element.199), kind=kOutput, calls=%fused_computation.3.clone.1 | convolution fusion | flops 2420637696 | bytes 1196032 | tf_op jit(solution)/shard_map/while/body/eval_jaxpr/gkr,gkc->grc/dot_general | solution.py:37
  147.0 7.5 %fusion.55 = f32[16,128,128]{2,1,0:T(8,128)S(1)} fusion(s32[16,768]{1,0:T(8,128)S(1)} %get-tuple-element.198, f32[16,768]{1,0:T(8,128)S(1)} %dynamic-slice_bitcast_fusion.6, s32[16,768]{1,0:T(8,128)S(1)} %get-tuple-element.199), kind=kOutput, calls=%fused_computation.3.clone.1 | convolution fusion | flops 2420637696 | bytes 1196032 | tf_op jit(solution)/shard_map/while/body/eval_jaxpr/gkr,gkc->grc/dot_general | solution.py:37
  157.0 7.5 %fusion.55 = f32[16,128,128]{2,1,0:T(8,128)S(1)} fusion(s32[16,768]{1,0:T(8,128)S(1)} %get-tuple-element.198, f32[16,768]{1,0:T(8,128)S(1)} %dynamic-slice_bitcast_fusion.6, s32[16,768]{1,0:T(8,128)S(1)} %get-tuple-element.199), kind=kOutput, calls=%fused_computation.3.clone.1 | convolution fusion | flops 2420637696 | bytes 1196032 | tf_op jit(solution)/shard_map/while/body/eval_jaxpr/gkr,gkc->grc/dot_general | solution.py:37
  167.0 7.5 %fusion.55 = f32[16,128,128]{2,1,0:T(8,128)S(1)} fusion(s32[16,768]{1,0:T(8,128)S(1)} %get-tuple-element.198, f32[16,768]{1,0:T(8,128)S(1)} %dynamic-slice_bitcast_fusion.6, s32[16,768]{1,0:T(8,128)S(1)} %get-tuple-element.199), kind=kOutput, calls=%fused_computation.3.clone.1 | convolution fusion | flops 2420637696 | bytes 1196032 | tf_op jit(solution)/shard_map/while/body/eval_jaxpr/gkr,gkc->grc/dot_general | solution.py:37
  176.9 7.5 %fusion.55 = f32[16,128,128]{2,1,0:T(8,128)S(1)} fusion(s32[16,768]{1,0:T(8,128)S(1)} %get-tuple-element.198, f32[16,768]{1,0:T(8,128)S(1)} %dynamic-slice_bitcast_fusion.6, s32[16,768]{1,0:T(8,128)S(1)} %get-tuple-element.199), kind=kOutput, calls=%fused_computation.3.clone.1 | convolution fusion | flops 2420637696 | bytes 1196032 | tf_op jit(solution)/shard_map/while/body/eval_jaxpr/gkr,gkc->grc/dot_general | solution.py:37
  186.9 7.5 %fusion.55 = f32[16,128,128]{2,1,0:T(8,128)S(1)} fusion(s32[16,768]{1,0:T(8,128)S(1)} %get-tuple-element.198, f32[16,768]{1,0:T(8,128)S(1)} %dynamic-slice_bitcast_fusion.6, s32[16,768]{1,0:T(8,128)S(1)} %get-tuple-element.199), kind=kOutput, calls=%fused_computation.3.clone.1 | convolution fusion | flops 2420637696 | bytes 1196032 | tf_op jit(solution)/shard_map/while/body/eval_jaxpr/gkr,gkc->grc/dot_general | solution.py:37
  206.8 7.5 %fusion.55 = f32[16,128,128]{2,1,0:T(8,128)S(1)} fusion(s32[16,768]{1,0:T(8,128)S(1)} %get-tuple-element.198, f32[16,768]{1,0:T(8,128)S(1)} %dynamic-slice_bitcast_fusion.6, s32[16,768]{1,0:T(8,128)S(1)} %get-tuple-element.199), kind=kOutput, calls=%fused_computation.3.clone.1 | convolution fusion | flops 2420637696 | bytes 1196032 | tf_op jit(solution)/shard_map/while/body/eval_jaxpr/gkr,gkc->grc/dot_general | solution.py:37
  216.8 7.5 %fusion.55 = f32[16,128,128]{2,1,0:T(8,128)S(1)} fusion(s32[16,768]{1,0:T(8,128)S(1)} %get-tuple-element.198, f32[16,768]{1,0:T(8,128)S(1)} %dynamic-slice_bitcast_fusion.6, s32[16,768]{1,0:T(8,128)S(1)} %get-tuple-element.199), kind=kOutput, calls=%fused_computation.3.clone.1 | convolution fusion | flops 2420637696 | bytes 1196032 | tf_op jit(solution)/shard_map/while/body/eval_jaxpr/gkr,gkc->grc/dot_general | solution.py:37
  226.7 7.5 %fusion.55 = f32[16,128,128]{2,1,0:T(8,128)S(1)} fusion(s32[16,768]{1,0:T(8,128)S(1)} %get-tuple-element.198, f32[16,768]{1,0:T(8,128)S(1)} %dynamic-slice_bitcast_fusion.6, s32[16,768]{1,0:T(8,128)S(1)} %get-tuple-element.199), kind=kOutput, calls=%fused_computation.3.clone.1 | convolution fusion | flops 2420637696 | bytes 1196032 | tf_op jit(solution)/shard_map/while/body/eval_jaxpr/gkr,gkc->grc/dot_general | solution.py:37
  246.7 7.5 %fusion.55 = f32[16,128,128]{2,1,0:T(8,128)S(1)} fusion(s32[16,768]{1,0:T(8,128)S(1)} %get-tuple-element.198, f32[16,768]{1,0:T(8,128)S(1)} %dynamic-slice_bitcast_fusion.6, s32[16,768]{1,0:T(8,128)S(1)} %get-tuple-element.199), kind=kOutput, calls=%fused_computation.3.clone.1 | convolution fusion | flops 2420637696 | bytes 1196032 | tf_op jit(solution)/shard_map/while/body/eval_jaxpr/gkr,gkc->grc/dot_general | solution.py:37
  256.6 7.5 %fusion.55 = f32[16,128,128]{2,1,0:T(8,128)S(1)} fusion(s32[16,768]{1,0:T(8,128)S(1)} %get-tuple-element.198, f32[16,768]{1,0:T(8,128)S(1)} %dynamic-slice_bitcast_fusion.6, s32[16,768]{1,0:T(8,128)S(1)} %get-tuple-element.199), kind=kOutput, calls=%fused_computation.3.clone.1 | convolution fusion | flops 2420637696 | bytes 1196032 | tf_op jit(solution)/shard_map/while/body/eval_jaxpr/gkr,gkc->grc/dot_general | solution.py:37
  266.6 7.5 %fusion.55 = f32[16,128,128]{2,1,0:T(8,128)S(1)} fusion(s32[16,768]{1,0:T(8,128)S(1)} %get-tuple-element.198, f32[16,768]{1,0:T(8,128)S(1)} %dynamic-slice_bitcast_fusion.6, s32[16,768]{1,0:T(8,128)S(1)} %get-tuple-element.199), kind=kOutput, calls=%fused_computation.3.clone.1 | convolution fusion | flops 2420637696 | bytes 1196032 | tf_op jit(solution)/shard_map/while/body/eval_jaxpr/gkr,gkc->grc/dot_general | solution.py:37
  286.5 7.5 %fusion.55 = f32[16,128,128]{2,1,0:T(8,128)S(1)} fusion(s32[16,768]{1,0:T(8,128)S(1)} %get-tuple-element.198, f32[16,768]{1,0:T(8,128)S(1)} %dynamic-slice_bitcast_fusion.6, s32[16,768]{1,0:T(8,128)S(1)} %get-tuple-element.199), kind=kOutput, calls=%fused_computation.3.clone.1 | convolution fusion | flops 2420637696 | bytes 1196032 | tf_op jit(solution)/shard_map/while/body/eval_jaxpr/gkr,gkc->grc/dot_general | solution.py:37
  296.5 7.5 %fusion.55 = f32[16,128,128]{2,1,0:T(8,128)S(1)} fusion(s32[16,768]{1,0:T(8,128)S(1)} %get-tuple-element.198, f32[16,768]{1,0:T(8,128)S(1)} %dynamic-slice_bitcast_fusion.6, s32[16,768]{1,0:T(8,128)S(1)} %get-tuple-element.199), kind=kOutput, calls=%fused_computation.3.clone.1 | convolution fusion | flops 2420637696 | bytes 1196032 | tf_op jit(solution)/shard_map/while/body/eval_jaxpr/gkr,gkc->grc/dot_general | solution.py:37
  306.4 7.5 %fusion.55 = f32[16,128,128]{2,1,0:T(8,128)S(1)} fusion(s32[16,768]{1,0:T(8,128)S(1)} %get-tuple-element.198, f32[16,768]{1,0:T(8,128)S(1)} %dynamic-slice_bitcast_fusion.6, s32[16,768]{1,0:T(8,128)S(1)} %get-tuple-element.199), kind=kOutput, calls=%fused_computation.3.clone.1 | convolution fusion | flops 2420637696 | bytes 1196032 | tf_op jit(solution)/shard_map/while/body/eval_jaxpr/gkr,gkc->grc/dot_general | solution.py:37
  316.7 30.6 %psum.56 = f32[512]{0:T(512)S(1)} all-reduce(f32[512]{0:T(512)S(1)} %bitcast.52), channel_id=1, replica_groups=mesh['row'=8,'col'=16] {'col'}, use_global_device_ids=true, to_apply=%region_6.7 | all-reduce | flops 512 | bytes 4096 | tf_op jit(solution)/shard_map/psum | solution.py:102
  347.9 20.5 %psum.57 = f32[]{:T(128)} all-reduce(f32[]{:T(128)} %reduce_sum.92), channel_id=1, replica_groups=mesh['row'=8,'col'=16] {'row'}, use_global_device_ids=true, to_apply=%region_8.9 | all-reduce | flops 1 | bytes 8 | tf_op jit(solution)/shard_map/psum | solution.py:66
  369.8 12.6 %psum.58 = f32[512]{0:T(512)S(1)} all-reduce(f32[512]{0:T(512)S(1)} %bitcast.53), channel_id=1, replica_groups=mesh['row'=8,'col'=16] {'row'}, use_global_device_ids=true, to_apply=%region_10.11 | all-reduce | flops 512 | bytes 4096 | tf_op jit(solution)/shard_map/psum | solution.py:107
  383.0 29.1 %psum.59 = f32[]{:T(128)} all-reduce(f32[]{:T(128)} %reduce_sum.95), channel_id=1, replica_groups=mesh['row'=8,'col'=16] {'col'}, use_global_device_ids=true, to_apply=%region_12.13 | all-reduce | flops 1 | bytes 8 | tf_op jit(solution)/shard_map/psum | solution.py:70
  420.2 30.2 %psum.60 = f32[512]{0:T(512)S(1)} all-reduce(f32[512]{0:T(512)S(1)} %bitcast.54), channel_id=1, replica_groups=mesh['row'=8,'col'=16] {'col'}, use_global_device_ids=true, to_apply=%region_14.15 | all-reduce | flops 512 | bytes 4096 | tf_op jit(solution)/shard_map/psum | solution.py:102
  451.0 27.3 %psum.61 = f32[]{:T(128)} all-reduce(f32[]{:T(128)} %reduce_sum.98), channel_id=1, replica_groups=mesh['row'=8,'col'=16] {'row'}, use_global_device_ids=true, to_apply=%region_16.17 | all-reduce | flops 1 | bytes 8 | tf_op jit(solution)/shard_map/psum | solution.py:66
  480.9 12.4 %psum.62 = f32[512]{0:T(512)S(1)} all-reduce(f32[512]{0:T(512)S(1)} %bitcast.51), channel_id=1, replica_groups=mesh['row'=8,'col'=16] {'row'}, use_global_device_ids=true, to_apply=%region_18.19 | all-reduce | flops 512 | bytes 4096 | tf_op jit(solution)/shard_map/psum | solution.py:107
  494.1 29.1 %psum.63 = f32[]{:T(128)} all-reduce(f32[]{:T(128)} %reduce_sum.101), channel_id=1, replica_groups=mesh['row'=8,'col'=16] {'col'}, use_global_device_ids=true, to_apply=%region_20.21 | all-reduce | flops 1 | bytes 8 | tf_op jit(solution)/shard_map/psum | solution.py:70
  (147 shorter events, 135.6 us)
Async XLA Ops:
  8.5 11.5 %copy-start = (f32[144,768]{1,0:T(8,128)S(1)}, f32[144,768]{1,0:T(8,128)}, u32[]{:S(2)}) copy-start(f32[144,768]{1,0:T(8,128)} %param.8) | copy-start | bytes 1327108
  8.6 11.5 %copy-start.1 = (s32[144]{0:T(256)S(1)}, s32[144]{0:T(256)}, u32[]{:S(2)}) copy-start(s32[144]{0:T(256)} %param.9) | copy-start | bytes 1732
  8.6 35.6 %all-to-all-start = ((s32[128,3,768]{2,1,0:T(4,128)}), s32[128,3,768]{2,1,0:T(4,128)S(1)}, u32[]{:S(2)}, u32[]{:S(2)}) async-start(s32[128,3,768]{2,1,0:T(4,128)} %broadcast_select_fusion.1), calls=%async_computation | async-start | bytes 3145728 | tf_op jit(solution)/shard_map/all_to_all | solution.py:60
  44.1 29.8 %all-to-all-start.1 = ((f32[128,3,768]{2,1,0:T(4,128)}), f32[128,3,768]{2,1,0:T(4,128)}, u32[]{:S(2)}, u32[]{:S(2)}) async-start(f32[128,3,768]{2,1,0:T(4,128)} %broadcast_select_fusion), calls=%async_computation.1 | async-start | bytes 3145728 | tf_op jit(solution)/shard_map/all_to_all | solution.py:61
where the time goes:
time: 534 us; the launch traced here: 526 us
  matrix products  218 us (41%)
  blocking collectives  192 us (36%)
  local copies, waits for them, and re-layouts  34.2 us (6%)
  waiting for transfers between devices  32.8 us (6%)
  other arithmetic  26.9 us (5%)
  starting transfers between devices  17.4 us (3%)
    dot_general x24, matrix products, add_group(): jnp.einsum('gkr,gkc->grc', row_hot, col_hot, precision=lax.Precision.HIGH...  179 us
    psum x2, blocking collectives, on_device(): row_sums = lax.psum(jnp.sum(balanced, axis=1), 'col')  60.8 us
    psum x2, blocking collectives, col_grand_total(): return lax.psum(jnp.sum(col_sums), 'col')  58.3 us
    psum x2, blocking collectives, row_grand_total(): return lax.psum(jnp.sum(row_sums), 'row')  47.8 us
    dot_general x24, matrix products, add_group(): jnp.einsum('gs,grc->src', choose, pieces, precision=lax.Precision.HIGHEST)  38.8 us
    psum x2, blocking collectives, on_device(): col_sums = lax.psum(jnp.sum(balanced, axis=0), 'row')  25 us
    broadcast_in_dim x24, local copies, waits for them, and re-layouts, add_group(): row_hot = jnp.where(rows_now[:, :, None] == lanes, wgt_now[:, :, None], 0.0)  19.4 us
    all_to_all x1, waiting for transfers between devices, deliver_owner(): lax.all_to_all(send_wgt, ('row', 'col'), split_axis=0, concat_axis=0, til...  16.8 us
  transfers between devices with their start and end apart: 2, of which 2 were waited for; matrix products, arithmetic and copies ran while one was open for 3% of the time, Pallas kernels for 0%

commit v1 on v0

v1 whole, which is shorter than its diff:
```python
import jax
import jax.numpy as jnp
from jax import lax
from jax.experimental import pallas as pl
from jax.experimental.pallas import tpu as pltpu
from jax.sharding import PartitionSpec as P

TILE = 512
SUB = 128
LANES = 128
SIDE = TILE // SUB
SWEEPS = 2

prior_count = 0.015625


def pack_kernel(tile_ref, counts_ref, rows_ref, cols_ref, wgt_ref, send_ref, seen_ref):
    blocks, cap = rows_ref.shape
    chunks = cap // LANES
    n_col = 16
    for i in range(seen_ref.shape[0]):
        seen_ref[i] = 0

    @pl.loop(0, blocks // 8)
    def _(group):
        at = pl.ds(pl.multiple_of(group * 8, 8), 8)
        place = (rows_ref[at, :] & (TILE - 1)) * TILE + (cols_ref[at, :] & (TILE - 1))
        place = place.astype(jnp.float32)
        wgt = wgt_ref[at, :]
        entry = lax.broadcasted_iota(jnp.int32, (1, cap), 1)
        for r in range(8):
            b = group * 8 + r
            tile = tile_ref[b]
            tile_row = tile // n_col
            tile_col = tile % n_col
            diagonal = tile_row == tile_col
            rank = jnp.where(diagonal, seen_ref[tile_row], 0)
            seen_ref[tile_row] = seen_ref[tile_row] + jnp.where(diagonal, 1, 0)
            dest = jnp.where(rank == 2, (tile_row ^ 1) * n_col + tile_col, tile)
            slot = jnp.minimum(rank, 1)
            kept = jnp.where(entry < counts_ref[b], wgt[r : r + 1, :], 0.0)
            parts = [place[r : r + 1, LANES * k : LANES * (k + 1)] for k in range(chunks)]
            parts += [kept[:, LANES * k : LANES * (k + 1)] for k in range(chunks)]
            base = slot * 2 * chunks
            for k, part in enumerate(parts):
                send_ref[dest, pl.ds(base + k, 1), :] = part


def pack(tile, counts, rows, cols, wgt, devices):
    blocks, cap = rows.shape
    return pl.pallas_call(
        pack_kernel,
        out_shape=jax.ShapeDtypeStruct((devices, 4 * cap // LANES, LANES), jnp.float32),
        in_specs=[pl.BlockSpec(memory_space=pltpu.SMEM)] * 2
        + [pl.BlockSpec(memory_space=pltpu.VMEM)] * 3,
        out_specs=pl.BlockSpec(memory_space=pltpu.VMEM),
        scratch_shapes=[pltpu.SMEM((8,), jnp.int32)],
        name="pack",
    )(tile, counts, rows, cols, wgt)


def square_of(x, chunks):
    place = x[:chunks].astype(jnp.int32)
    wgt = x[chunks:]
    local_row = ((place >> 9) & (SUB - 1)).astype(jnp.float32)
    local_col = (place & (SUB - 1)).astype(jnp.float32)
    high = wgt.astype(jnp.bfloat16).astype(jnp.float32)
    rest = wgt - high
    bins = lax.broadcasted_iota(jnp.int32, (SUB, LANES), 0).astype(jnp.bfloat16)
    one = jnp.ones((SUB, LANES), jnp.bfloat16)
    zero = jnp.zeros((SUB, LANES), jnp.bfloat16)

    def spread(v, k):
        return jnp.broadcast_to(v[k : k + 1], (SUB, LANES)).astype(jnp.bfloat16)

    row_hot, high_hot, rest_hot = [], [], []
    for k in range(chunks):
        row_hot.append(jnp.where(spread(local_row, k) == bins, one, zero))
        hit = spread(local_col, k) == bins
        high_hot.append(jnp.where(hit, spread(high, k), zero))
        rest_hot.append(jnp.where(hit, spread(rest, k), zero))
    row_hot = jnp.concatenate(row_hot, axis=1)
    col_hot = jnp.concatenate(
        [jnp.concatenate(high_hot, axis=1), jnp.concatenate(rest_hot, axis=1)], axis=0
    )
    both = lax.dot_general(
        row_hot, col_hot, (((1,), (1,)), ((), ())), preferred_element_type=jnp.float32
    )
    return both[:, :SUB] + both[:, SUB:]


def add_blocks(got_ref, slot, acc_ref, unroll):
    sources = got_ref.shape[0]
    chunks = got_ref.shape[1] // 4

    @pl.loop(0, sources // unroll)
    def _(step):
        for u in range(unroll):
            x = got_ref[step * unroll + u, 2 * chunks * slot : 2 * chunks * (slot + 1), :]
            head = x[0, 0].astype(jnp.int32)
            square = (head >> 16) * SIDE + ((head >> 7) & (SIDE - 1))
            acc_ref[square] += square_of(x, chunks)


def write_tile(acc_ref, out_ref):
    for i in range(SIDE):
        for j in range(SIDE):
            out_ref[SUB * i : SUB * (i + 1), SUB * j : SUB * (j + 1)] = acc_ref[i * SIDE + j]


def extra_kernel(got_ref, out_ref, acc_ref):
    me_row = lax.axis_index("row")
    me_col = lax.axis_index("col")
    step = pl.program_id(0)

    @pl.when((me_row // 2) == (me_col // 2))
    def _():
        @pl.when(step == 0)
        def _():
            acc_ref[...] = jnp.zeros_like(acc_ref)

        add_blocks(got_ref, 1, acc_ref, 4)

        @pl.when(step == pl.num_programs(0) - 1)
        def _():
            write_tile(acc_ref, out_ref)


def main_kernel(got_ref, extra_ref, out_ref, acc_ref):
    me_row = lax.axis_index("row")
    me_col = lax.axis_index("col")
    step = pl.program_id(0)

    @pl.when(step == 0)
    def _():
        acc_ref[...] = jnp.zeros_like(acc_ref)

    add_blocks(got_ref, 0, acc_ref, 4)

    @pl.when(step == pl.num_programs(0) - 1)
    def _():
        write_tile(acc_ref, out_ref)

        @pl.when(me_row == me_col)
        def _():
            out_ref[...] += extra_ref[...]


bin_steps = 8


def bin_extra(got):
    sources = got.shape[0]
    return pl.pallas_call(
        extra_kernel,
        grid=(bin_steps,),
        out_shape=jax.ShapeDtypeStruct((TILE, TILE), jnp.float32),
        in_specs=[pl.BlockSpec((sources // bin_steps,) + got.shape[1:], lambda i: (i, 0, 0))],
        out_specs=pl.BlockSpec((TILE, TILE), lambda i: (0, 0)),
        scratch_shapes=[pltpu.VMEM((SIDE * SIDE, SUB, SUB), jnp.float32)],
        name="bin_extra",
    )(got)


def bin_main(got, extra):
    sources = got.shape[0]
    return pl.pallas_call(
        main_kernel,
        grid=(bin_steps,),
        out_shape=jax.ShapeDtypeStruct((TILE, TILE), jnp.float32),
        in_specs=[
            pl.BlockSpec((sources // bin_steps,) + got.shape[1:], lambda i: (i, 0, 0)),
            pl.BlockSpec((TILE, TILE), lambda i: (0, 0)),
        ],
        out_specs=pl.BlockSpec((TILE, TILE), lambda i: (0, 0)),
        scratch_shapes=[pltpu.VMEM((SIDE * SIDE, SUB, SUB), jnp.float32)],
        name="bin_main",
    )(got, extra)


def to_lanes(column):
    return jnp.concatenate(
        [
            jnp.sum(jnp.where(same_lane(), column[LANES * k : LANES * (k + 1)], 0.0), axis=0, keepdims=True)
            for k in range(TILE // LANES)
        ],
        axis=0,
    )


def same_lane():
    down = lax.broadcasted_iota(jnp.int32, (LANES, LANES), 0)
    across = lax.broadcasted_iota(jnp.int32, (LANES, LANES), 1)
    return down == across


def to_column(vec):
    return jnp.concatenate(
        [
            jnp.sum(jnp.where(same_lane(), vec[k : k + 1], 0.0), axis=1, keepdims=True)
            for k in range(vec.shape[0])
        ],
        axis=0,
    )


def as_row(vec):
    return jnp.concatenate([vec[k : k + 1] for k in range(vec.shape[0])], axis=1)


def from_row(row):
    return jnp.concatenate(
        [row[:, LANES * k : LANES * (k + 1)] for k in range(TILE // LANES)], axis=0
    )


def first_kernel(part_ref, moved_ref, tile_ref, rows_ref):
    tile = part_ref[...] + moved_ref[...] + prior_count
    tile_ref[...] = tile
    sums = to_lanes(jnp.sum(tile, axis=1, keepdims=True))
    for d in range(rows_ref.shape[0]):
        rows_ref[d] = sums


def down_first_kernel(tile_ref, got_ref, out_ref):
    row_sums = jnp.sum(got_ref[...], axis=0)
    total = jnp.sum(row_sums, axis=1, keepdims=True)
    sums = from_row(jnp.sum(tile_ref[...] / to_column(row_sums), axis=0, keepdims=True))
    send = jnp.concatenate([sums, jnp.broadcast_to(total, sums.shape)], axis=0)
    for d in range(out_ref.shape[0]):
        out_ref[d] = send


def across_kernel(tile_ref, got_ref, out_ref):
    vec = jnp.sum(got_ref[:, : TILE // LANES, :], axis=0) * 2.0
    sums = to_lanes(jnp.sum(tile_ref[...] / as_row(vec), axis=1, keepdims=True))
    for d in range(out_ref.shape[0]):
        out_ref[d] = sums


def down_kernel(tile_ref, got_ref, out_ref):
    vec = jnp.sum(got_ref[...], axis=0)
    sums = from_row(jnp.sum(tile_ref[...] / to_column(vec), axis=0, keepdims=True))
    for d in range(out_ref.shape[0]):
        out_ref[d] = sums


def last_kernel(r_bins, tile_ref, first_ref, across_ref, down_ref, out_ref, row_ref, col_ref):
    total = jnp.sum(first_ref[:, TILE // LANES :, 0:1], axis=(0, 1), keepdims=True)[0]
    row_mean = total / r_bins
    row_bias = jnp.sum(across_ref[...], axis=0) / row_mean
    col_bias = jnp.sum(down_ref[...], axis=0) * 2.0
    row_ref[...] = row_bias
    col_ref[...] = col_bias
    out_ref[...] = tile_ref[...] / (to_column(row_bias) * as_row(col_bias))


def on_device(pair_rows, pair_cols, pair_weights, block_counts):
    n_row = lax.axis_size("row")
    n_col = lax.axis_size("col")
    devices = n_row * n_col
    r_bins = float(TILE * n_row)
    lines = TILE // LANES
    tile_id = (pair_rows[:, 0] >> 9) * n_col + (pair_cols[:, 0] >> 9)
    send = pack(tile_id, block_counts, pair_rows, pair_cols, pair_weights, devices)
    got = lax.all_to_all(send, ("row", "col"), split_axis=0, concat_axis=0, tiled=True)
    extra = bin_extra(got)
    handed = [((r ^ 1) * n_col + r, r * n_col + r) for r in range(n_row)]
    moved = lax.ppermute(extra, ("row", "col"), handed)
    part = bin_main(got, extra)
    tile_type = jax.ShapeDtypeStruct((TILE, TILE), jnp.float32)
    vec_type = jax.ShapeDtypeStruct((lines, LANES), jnp.float32)

    def sent(n, k=lines):
        return jax.ShapeDtypeStruct((n, k, LANES), jnp.float32)

    def swap(x, axis):
        return lax.all_to_all(x, axis, split_axis=0, concat_axis=0, tiled=True)

    tile, rows_part = pl.pallas_call(first_kernel, out_shape=(tile_type, sent(n_col)), name="first")(part, moved)
    rows_got = swap(rows_part, "col")
    first_part = pl.pallas_call(down_first_kernel, out_shape=sent(n_row, 2 * lines), name="down_first")(tile, rows_got)
    first_got = swap(first_part, "row")
    across_part = pl.pallas_call(across_kernel, out_shape=sent(n_col), name="across")(tile, first_got)
    across_got = swap(across_part, "col")
    down_part = pl.pallas_call(down_kernel, out_shape=sent(n_row), name="down")(tile, across_got)
    down_got = swap(down_part, "row")
    balanced, row_bias, col_bias = pl.pallas_call(
        lambda *refs: last_kernel(r_bins, *refs), out_shape=(tile_type, vec_type, vec_type), name="last"
    )(tile, first_got, across_got, down_got)
    return (balanced, row_bias.reshape(-1), col_bias.reshape(-1))


def solution(mesh):
    return jax.shard_map(
        on_device,
        mesh=mesh,
        in_specs=(
            P(("row", "col"), None),
            P(("row", "col"), None),
            P(("row", "col"), None),
            P(("row", "col")),
        ),
        out_specs=(P("row", "col"), P("row"), P("col")),
        check_vma=False,
    )
```

time: 534 us -> 148 us (0.28); the launches traced: 526 us -> 147 us
  matrix products: 218 us -> 0 us
  blocking collectives: 192 us -> 76.5 us
  Pallas kernels: 0 us -> 64 us
  local copies, waits for them, and re-layouts: 34.2 us -> 0.97 us
  waiting for transfers between devices: 32.8 us -> 0.01 us
  other arithmetic: 26.9 us -> 1.6 us
  starting transfers between devices: 17.4 us -> 3.41 us
    dot_general x48 -> x0, matrix products: 218 us -> none  [the longest x24 179 us: add_group(): jnp.einsum('gkr,gkc->grc', row_hot, col_hot, precision=lax.Precision.HIGH...]
    psum x8 -> x0, blocking collectives: 192 us -> none  [the longest x2 60.8 us: on_device(): row_sums = lax.psum(jnp.sum(balanced, axis=1), 'col')]
    all_to_all x0 -> x5, blocking collectives: none -> 76.5 us  [the longest x4 40.8 us: swap(): return lax.all_to_all(x, axis, split_axis=0, concat_axis=0, tiled=True)]
    pallas_call x0 -> x8, Pallas kernels: none -> 64 us  [the longest x1 24.2 us: bin_main(): pl.pallas_call(main_kernel, grid=(bin_steps,), out_shape=jax.ShapeDtypeSt...]
    all_to_all x2 -> x0, waiting for transfers between devices: 32.8 us -> none  [the longest x1 16.8 us: deliver_owner(): lax.all_to_all(send_wgt, ('row', 'col'), split_axis=0, concat_axis=0, til...]
    broadcast_in_dim x25 -> x0, local copies, waits for them, and re-layouts: 19.6 us -> none  [the longest x24 19.4 us: add_group(): row_hot = jnp.where(rows_now[:, :, None] == lanes, wgt_now[:, :, None], 0.0)]
    all_to_all x2 -> x0, starting transfers between devices: 17.4 us -> none  [the longest x1 11.5 us: deliver_owner(): lax.all_to_all(send_pos, ('row', 'col'), split_axis=0, concat_axis=0, til...]
    reduce_sum x9 -> x0, other arithmetic: 13.2 us -> none  [the longest x2 8.5 us: on_device(): row_sums = lax.psum(jnp.sum(balanced, axis=1), 'col')]
  transfers between devices with their start and end apart: 2 -> 1, of which waited for: 2 -> 0; matrix products, arithmetic and copies ran while one was open for 3% -> 0% of each run, Pallas kernels for 0% -> 16%
where the time goes in v1:
time: 148 us; the launch traced here: 147 us
  blocking collectives  76.5 us (52%)
  Pallas kernels  64 us (43%)
  starting transfers between devices  3.41 us (2%)
  other arithmetic  1.6 us (1%)
    all_to_all x4, blocking collectives, swap(): return lax.all_to_all(x, axis, split_axis=0, concat_axis=0, tiled=True)  40.8 us
    all_to_all x1, blocking collectives, on_device(): lax.all_to_all(send, ('row', 'col'), split_axis=0, concat_axis=0, tiled=T...  35.7 us
    pallas_call x1, Pallas kernels, bin_main(): pl.pallas_call(main_kernel, grid=(bin_steps,), out_shape=jax.ShapeDtypeSt...  24.2 us
    pallas_call x1, Pallas kernels, bin_extra(): pl.pallas_call(extra_kernel, grid=(bin_steps,), out_shape=jax.ShapeDtypeS...  23.9 us
    pallas_call x1, Pallas kernels, pack(): pl.pallas_call(pack_kernel, out_shape=jax.ShapeDtypeStruct((devices, 4 *...  4.38 us
    ppermute x1, starting transfers between devices, on_device(): moved = lax.ppermute(extra, ('row', 'col'), handed)  3.41 us
  transfers between devices with their start and end apart: 1, of which 0 were waited for; matrix products, arithmetic and copies ran while one was open for 0% of the time, Pallas kernels for 16%

profile of v1, /device:TPU:1, one launch (start us, length us, event | category | flops | bytes accessed | tf_op | source)
XLA Modules:
  0.0 147.1 jit_solution(15672356601794675180)
XLA Ops:
  0.6 1.6 %add_reduce_fusion.tile_ref = s32[144]{0:T(256)} fusion(s32[144,768]{1,0:T(8,128)} %cols_ref.1, s32[144,768]{1,0:T(8,128)} %rows_ref.1), kind=kLoop, calls=%fused_computation | loop fusion | flops 576 | bytes 1728 | tf_op jit(solution)/shard_map/add | solution.py:264
  2.2 4.4 %pack.1 = f32[128,24,128]{2,1,0:T(8,128)} custom-call(s32[144]{0:T(256)} %add_reduce_fusion.tile_ref, s32[144]{0:T(256)} %counts_ref.1, s32[144,768]{1,0:T(8,128)} %rows_ref.1, s32[144,768]{1,0:T(8,128)} %cols_ref.1, f32[144,768]{1,0:T(8,128)} %wgt_ref.1), custom_call_target="tpu_custom_call" | custom-call | tf_op jit(solution)/shard_map/pack/pallas_call | solution.py:51
  6.6 35.7 %all_to_all.25.got_ref = f32[128,24,128]{2,1,0:T(8,128)} all-to-all(f32[128,24,128]{2,1,0:T(8,128)} %pack.1), channel_id=1, replica_groups=mesh['row'=8,'col'=16] {'row','col'}, dimensions={0} | all-to-all | bytes 3145728 | tf_op jit(solution)/shard_map/all_to_all | solution.py:266
  42.3 23.9 %bin_extra.1.extra_ref = f32[512,512]{1,0:T(8,128)} custom-call(f32[128,24,128]{2,1,0:T(8,128)} %all_to_all.25.got_ref), custom_call_target="tpu_custom_call" | custom-call | tf_op jit(solution)/shard_map/bin_extra/pallas_call | solution.py:154
  66.2 3.4 %collective-permute-start = (f32[512,512]{1,0:T(8,128)}, f32[512,512]{1,0:T(8,128)S(1)}, u32[]{:S(2)}, u32[]{:S(2)}) collective-permute-start(f32[512,512]{1,0:T(8,128)} %bin_extra.1.extra_ref), channel_id=1, source_target_pairs={{16,0},{1,17},{50,34},{35,51},{84,68},{69,85},{118,102},{103,119}} | collective-permute-start | bytes 3145736 | tf_op jit(solution)/shard_map/ppermute | solution.py:269
  69.6 24.2 %bin_main.1.part_ref = f32[512,512]{1,0:T(8,128)} custom-call(f32[128,24,128]{2,1,0:T(8,128)} %all_to_all.25.got_ref, f32[512,512]{1,0:T(8,128)} %bin_extra.1.extra_ref), custom_call_target="tpu_custom_call" | custom-call | tf_op jit(solution)/shard_map/bin_main/pallas_call | solution.py:167
  93.9 0.0 collective-permute-done.moved_ref
  93.9 0.0 copy-start
  93.9 1.0 copy-done
  94.8 2.6 %first.1 = (f32[512,512]{1,0:T(8,128)}, f32[16,4,128]{2,1,0:T(4,128)}) custom-call(f32[512,512]{1,0:T(8,128)} %bin_main.1.part_ref, f32[512,512]{1,0:T(8,128)} %copy-done), custom_call_target="tpu_custom_call" | custom-call | tf_op jit(solution)/shard_map/first/pallas_call | solution.py:280
  97.5 10.7 %all_to_all.26.got_ref = f32[16,4,128]{2,1,0:T(4,128)} all-to-all(f32[16,4,128]{2,1,0:T(4,128)} %get-tuple-element.9), channel_id=1, replica_groups=mesh['row'=8,'col'=16] {'col'}, dimensions={0} | all-to-all | bytes 65536 | tf_op jit(solution)/shard_map/all_to_all | solution.py:278
  108.2 2.1 %down_first.1 = f32[8,8,128]{2,1,0:T(8,128)} custom-call(f32[512,512]{1,0:T(8,128)} %get-tuple-element.8.tile_ref.refs_0_, f32[16,4,128]{2,1,0:T(4,128)} %all_to_all.26.got_ref), custom_call_target="tpu_custom_call" | custom-call | tf_op jit(solution)/shard_map/down_first/pallas_call | solution.py:282
  110.3 9.0 %all_to_all.27.got_ref.refs_1_ = f32[8,8,128]{2,1,0:T(8,128)} all-to-all(f32[8,8,128]{2,1,0:T(8,128)} %down_first.1), channel_id=1, replica_groups=mesh['row'=8,'col'=16] {'row'}, dimensions={0} | all-to-all | bytes 65536 | tf_op jit(solution)/shard_map/all_to_all | solution.py:278
  119.4 2.0 %across.1 = f32[16,4,128]{2,1,0:T(4,128)} custom-call(f32[512,512]{1,0:T(8,128)} %get-tuple-element.8.tile_ref.refs_0_, f32[8,8,128]{2,1,0:T(8,128)} %all_to_all.27.got_ref.refs_1_), custom_call_target="tpu_custom_call" | custom-call | tf_op jit(solution)/shard_map/across/pallas_call | solution.py:284
  121.4 10.6 %all_to_all.28.got_ref.refs_2_ = f32[16,4,128]{2,1,0:T(4,128)} all-to-all(f32[16,4,128]{2,1,0:T(4,128)} %across.1), channel_id=1, replica_groups=mesh['row'=8,'col'=16] {'col'}, dimensions={0} | all-to-all | bytes 65536 | tf_op jit(solution)/shard_map/all_to_all | solution.py:278
  131.9 2.1 %down.1 = f32[8,4,128]{2,1,0:T(4,128)} custom-call(f32[512,512]{1,0:T(8,128)} %get-tuple-element.8.tile_ref.refs_0_, f32[16,4,128]{2,1,0:T(4,128)} %all_to_all.28.got_ref.refs_2_), custom_call_target="tpu_custom_call" | custom-call | tf_op jit(solution)/shard_map/down/pallas_call | solution.py:286
  134.1 10.4 %all_to_all.29.refs_3_ = f32[8,4,128]{2,1,0:T(4,128)} all-to-all(f32[8,4,128]{2,1,0:T(4,128)} %down.1), channel_id=1, replica_groups=mesh['row'=8,'col'=16] {'row'}, dimensions={0} | all-to-all | bytes 32768 | tf_op jit(solution)/shard_map/all_to_all | solution.py:278
  144.5 2.6 %last.1 = (f32[512,512]{1,0:T(8,128)}, f32[4,128]{1,0:T(4,128)}, f32[4,128]{1,0:T(4,128)}) custom-call(f32[512,512]{1,0:T(8,128)} %get-tuple-element.8.tile_ref.refs_0_, f32[8,8,128]{2,1,0:T(8,128)} %all_to_all.27.got_ref.refs_1_, f32[16,4,128]{2,1,0:T(4,128)} %all_to_all.28.got_ref.refs_2_, f32[8,4,128]{2,1,0:T(4,128)} %all_to_all.29.refs_3_), custom_call_target="tpu_custom_call" | custom-call | tf_op jit(solution)/shard_map/last/pallas_call | solution.py:288
Async XLA Ops:
  66.2 27.7 %collective-permute-start = (f32[512,512]{1,0:T(8,128)}, f32[512,512]{1,0:T(8,128)S(1)}, u32[]{:S(2)}, u32[]{:S(2)}) collective-permute-start(f32[512,512]{1,0:T(8,128)} %bin_extra.1.extra_ref), channel_id=1, source_target_pairs={{16,0},{1,17},{50,34},{35,51},{84,68},{69,85},{118,102},{103,119}} | collective-permute-start | bytes 3145736 | tf_op jit(solution)/shard_map/ppermute | solution.py:269
  93.9 1.0 copy-start

commit v2 on v1

--- a/solution.py
+++ b/solution.py
@@ -14,7 +14,7 @@
 prior_count = 0.015625
 
 
-def pack_kernel(tile_ref, counts_ref, rows_ref, cols_ref, wgt_ref, send_ref, seen_ref):
+def pack_kernel(counts_ref, rows_ref, cols_ref, wgt_ref, send_ref, kept_ref, seen_ref):
     blocks, cap = rows_ref.shape
     chunks = cap // LANES
     n_col = 16
@@ -24,13 +24,19 @@
     @pl.loop(0, blocks // 8)
     def _(group):
         at = pl.ds(pl.multiple_of(group * 8, 8), 8)
-        place = (rows_ref[at, :] & (TILE - 1)) * TILE + (cols_ref[at, :] & (TILE - 1))
-        place = place.astype(jnp.float32)
-        wgt = wgt_ref[at, :]
-        entry = lax.broadcasted_iota(jnp.int32, (1, cap), 1)
+        rows = rows_ref[at, :]
+        cols = cols_ref[at, :]
+        place = ((rows & (TILE - 1)) * TILE + (cols & (TILE - 1))).astype(jnp.float32)
+        tiles = (rows[:, :1] // TILE) * n_col + cols[:, :1] // TILE
+        entry = lax.broadcasted_iota(jnp.int32, (8, cap), 1)
+        line = lax.broadcasted_iota(jnp.int32, (8, cap), 0)
+        count = jnp.zeros((8, cap), jnp.int32)
         for r in range(8):
-            b = group * 8 + r
-            tile = tile_ref[b]
+            count = jnp.where(line == r, counts_ref[group * 8 + r], count)
+        kept = jnp.where(entry < count, wgt_ref[at, :], 0.0)
+        kept_ref[at, :] = kept
+        for r in range(8):
+            tile = tiles[r, 0]
             tile_row = tile // n_col
             tile_col = tile % n_col
             diagonal = tile_row == tile_col
@@ -38,25 +44,64 @@
             seen_ref[tile_row] = seen_ref[tile_row] + jnp.where(diagonal, 1, 0)
             dest = jnp.where(rank == 2, (tile_row ^ 1) * n_col + tile_col, tile)
             slot = jnp.minimum(rank, 1)
-            kept = jnp.where(entry < counts_ref[b], wgt[r : r + 1, :], 0.0)
-            parts = [place[r : r + 1, LANES * k : LANES * (k + 1)] for k in range(chunks)]
-            parts += [kept[:, LANES * k : LANES * (k + 1)] for k in range(chunks)]
+            parts = [
+                x[r : r + 1, LANES * k : LANES * (k + 1)] for x in (place, kept) for k in range(chunks)
+            ]
             base = slot * 2 * chunks
             for k, part in enumerate(parts):
                 send_ref[dest, pl.ds(base + k, 1), :] = part
 
 
-def pack(tile, counts, rows, cols, wgt, devices):
+def pack(counts, rows, cols, wgt, devices):
     blocks, cap = rows.shape
     return pl.pallas_call(
         pack_kernel,
-        out_shape=jax.ShapeDtypeStruct((devices, 4 * cap // LANES, LANES), jnp.float32),
-        in_specs=[pl.BlockSpec(memory_space=pltpu.SMEM)] * 2
-        + [pl.BlockSpec(memory_space=pltpu.VMEM)] * 3,
-        out_specs=pl.BlockSpec(memory_space=pltpu.VMEM),
+        out_shape=(
+            jax.ShapeDtypeStruct((devices, 4 * cap // LANES, LANES), jnp.float32),
+            jax.ShapeDtypeStruct(wgt.shape, jnp.float32),
+        ),
+        in_specs=[pl.BlockSpec(memory_space=pltpu.SMEM)] + [pl.BlockSpec(memory_space=pltpu.VMEM)] * 3,
+        out_specs=(pl.BlockSpec(memory_space=pltpu.VMEM),) * 2,
         scratch_shapes=[pltpu.SMEM((8,), jnp.int32)],
         name="pack",
-    )(tile, counts, rows, cols, wgt)
+    )(counts, rows, cols, wgt)
+
+
+def row_share_kernel(n_col, rows_ref, kept_ref, out_ref, acc_ref):
+    blocks, cap = rows_ref.shape
+    acc_ref[...] = jnp.zeros_like(acc_ref)
+    bins = lax.broadcasted_iota(jnp.int32, (SUB, LANES), 0)
+
+    @pl.loop(0, blocks // 8)
+    def _(group):
+        at = pl.ds(pl.multiple_of(group * 8, 8), 8)
+        rows = rows_ref[at, :]
+        kept = kept_ref[at, :]
+        local = rows & (SUB - 1)
+        strips = rows[:, :1] // SUB
+        for r in range(8):
+            total = jnp.zeros((SUB, LANES), jnp.float32)
+            for k in range(cap // LANES):
+                lanes = slice(LANES * k, LANES * (k + 1))
+                total += jnp.where(local[r : r + 1, lanes] == bins, kept[r : r + 1, lanes], 0.0)
+            acc_ref[strips[r, 0]] += total
+
+    for strip in range(acc_ref.shape[0]):
+        column = jnp.sum(acc_ref[strip], axis=1, keepdims=True)
+        sums = jnp.sum(jnp.where(same_lane(), column, 0.0), axis=0, keepdims=True)
+        row, line = divmod(strip, TILE // SUB)
+        for c in range(n_col):
+            out_ref[row * n_col + c, line : line + 1, :] = sums
+
+
+def row_share(rows, kept, n_row, n_col):
+    return pl.pallas_call(
+        lambda *refs: row_share_kernel(n_col, *refs),
+        out_shape=jax.ShapeDtypeStruct((n_row * n_col, TILE // LANES, LANES), jnp.float32),
+        scratch_shapes=[pltpu.VMEM((n_row * TILE // SUB, SUB, LANES), jnp.float32)],
+        cost_estimate=pl.CostEstimate(flops=10**9, bytes_accessed=10**6, transcendentals=0),
+        name="row_share",
+    )(rows, kept)
 
 
 def square_of(x, chunks):
@@ -119,7 +164,7 @@
         def _():
             acc_ref[...] = jnp.zeros_like(acc_ref)
 
-        add_blocks(got_ref, 1, acc_ref, 4)
+        add_blocks(got_ref, 1, acc_ref, bin_unroll)
 
         @pl.when(step == pl.num_programs(0) - 1)
         def _():
@@ -135,7 +180,7 @@
     def _():
         acc_ref[...] = jnp.zeros_like(acc_ref)
 
-    add_blocks(got_ref, 0, acc_ref, 4)
+    add_blocks(got_ref, 0, acc_ref, bin_unroll)
 
     @pl.when(step == pl.num_programs(0) - 1)
     def _():
@@ -146,7 +191,9 @@
             out_ref[...] += extra_ref[...]
 
 
-bin_steps = 8
+bin_steps = 4
+bin_unroll = 8
+bin_cost = pl.CostEstimate(flops=10**10, bytes_accessed=2 * 10**6, transcendentals=0)
 
 
 def bin_extra(got):
@@ -158,6 +205,7 @@
         in_specs=[pl.BlockSpec((sources // bin_steps,) + got.shape[1:], lambda i: (i, 0, 0))],
         out_specs=pl.BlockSpec((TILE, TILE), lambda i: (0, 0)),
         scratch_shapes=[pltpu.VMEM((SIDE * SIDE, SUB, SUB), jnp.float32)],
+        cost_estimate=bin_cost,
         name="bin_extra",
     )(got)
 
@@ -174,6 +222,7 @@
         ],
         out_specs=pl.BlockSpec((TILE, TILE), lambda i: (0, 0)),
         scratch_shapes=[pltpu.VMEM((SIDE * SIDE, SUB, SUB), jnp.float32)],
+        cost_estimate=bin_cost,
         name="bin_main",
     )(got, extra)
 
@@ -214,79 +263,81 @@
     )
 
 
-def first_kernel(part_ref, moved_ref, tile_ref, rows_ref):
+def first_kernel(c_bins, part_ref, moved_ref, got_ref, tile_ref, out_ref):
     tile = part_ref[...] + moved_ref[...] + prior_count
     tile_ref[...] = tile
-    sums = to_lanes(jnp.sum(tile, axis=1, keepdims=True))
-    for d in range(rows_ref.shape[0]):
-        rows_ref[d] = sums
-
-
-def down_first_kernel(tile_ref, got_ref, out_ref):
-    row_sums = jnp.sum(got_ref[...], axis=0)
+    row_sums = jnp.sum(got_ref[...], axis=0) + c_bins * prior_count
     total = jnp.sum(row_sums, axis=1, keepdims=True)
-    sums = from_row(jnp.sum(tile_ref[...] / to_column(row_sums), axis=0, keepdims=True))
+    sums = from_row(jnp.sum(tile * to_column(1.0 / row_sums), axis=0, keepdims=True))
     send = jnp.concatenate([sums, jnp.broadcast_to(total, sums.shape)], axis=0)
     for d in range(out_ref.shape[0]):
         out_ref[d] = send
 
 
-def across_kernel(tile_ref, got_ref, out_ref):
-    vec = jnp.sum(got_ref[:, : TILE // LANES, :], axis=0) * 2.0
-    sums = to_lanes(jnp.sum(tile_ref[...] / as_row(vec), axis=1, keepdims=True))
+def across_kernel(wider, tile_ref, got_ref, out_ref):
+    vec = jnp.sum(got_ref[:, : TILE // LANES, :], axis=0) * wider
+    sums = to_lanes(jnp.sum(tile_ref[...] * as_row(1.0 / vec), axis=1, keepdims=True))
     for d in range(out_ref.shape[0]):
         out_ref[d] = sums
 
 
 def down_kernel(tile_ref, got_ref, out_ref):
     vec = jnp.sum(got_ref[...], axis=0)
-    sums = from_row(jnp.sum(tile_ref[...] / to_column(vec), axis=0, keepdims=True))
+    sums = from_row(jnp.sum(tile_ref[...] * to_column(1.0 / vec), axis=0, keepdims=True))
     for d in range(out_ref.shape[0]):
         out_ref[d] = sums
 
 
-def last_kernel(r_bins, tile_ref, first_ref, across_ref, down_ref, out_ref, row_ref, col_ref):
+def last_kernel(r_bins, wider, tile_ref, first_ref, across_ref, down_ref, out_ref, row_ref, col_ref):
     total = jnp.sum(first_ref[:, TILE // LANES :, 0:1], axis=(0, 1), keepdims=True)[0]
     row_mean = total / r_bins
     row_bias = jnp.sum(across_ref[...], axis=0) / row_mean
-    col_bias = jnp.sum(down_ref[...], axis=0) * 2.0
+    col_bias = jnp.sum(down_ref[...], axis=0) * wider
     row_ref[...] = row_bias
     col_ref[...] = col_bias
-    out_ref[...] = tile_ref[...] / (to_column(row_bias) * as_row(col_bias))
+    out_ref[...] = tile_ref[...] * to_column(1.0 / row_bias) * as_row(1.0 / col_bias)
 
 
 def on_device(pair_rows, pair_cols, pair_weights, block_counts):
     n_row = lax.axis_size("row")
     n_col = lax.axis_size("col")
-    devices = n_row * n_col
+    both = ("row", "col")
     r_bins = float(TILE * n_row)
+    c_bins = float(TILE * n_col)
+    wider = c_bins / r_bins
     lines = TILE // LANES
-    tile_id = (pair_rows[:, 0] >> 9) * n_col + (pair_cols[:, 0] >> 9)
-    send = pack(tile_id, block_counts, pair_rows, pair_cols, pair_weights, devices)
-    got = lax.all_to_all(send, ("row", "col"), split_axis=0, concat_axis=0, tiled=True)
+    tile_type = jax.ShapeDtypeStruct((TILE, TILE), jnp.float32)
+    vec_type = jax.ShapeDtypeStruct((lines, LANES), jnp.float32)
+
+    def sent(n, k=lines):
+        return jax.ShapeDtypeStruct((n, k, LANES), jnp.float32)
+
+    def swap(x, axis):
+        return lax.all_to_all(x, axis, split_axis=0, concat_axis=0, tiled=True)
+
+    send, kept = pack(block_counts, pair_rows, pair_cols, pair_weights, n_row * n_col)
+    got = swap(send, both)
+    share = row_share(pair_rows, kept, n_row, n_col)
+    shares = swap(share, both)
     extra = bin_extra(got)
     handed = [((r ^ 1) * n_col + r, r * n_col + r) for r in range(n_row)]
-    moved = lax.ppermute(extra, ("row", "col"), handed)
+    moved = lax.ppermute(extra, both, handed)
     part = bin_main(got, extra)
-    tile_type = jax.ShapeDtypeStruct((TILE, TILE), jnp.float32)
-    vec_type = jax.ShapeDtypeStruct((lines, LANES), jnp.float32)
-
-    def sent(n, k=lines):
-        return jax.ShapeDtypeStruct((n, k, LANES), jnp.float32)
-
-    def swap(x, axis):
-        return lax.all_to_all(x, axis, split_axis=0, concat_axis=0, tiled=True)
-
-    tile, rows_part = pl.pallas_call(first_kernel, out_shape=(tile_type, sent(n_col)), name="first")(part, moved)
-    rows_got = swap(rows_part, "col")
-    first_part = pl.pallas_call(down_first_kernel, out_shape=sent(n_row, 2 * lines), name="down_first")(tile, rows_got)
+
+    tile, first_part = pl.pallas_call(
+        lambda *refs: first_kernel(c_bins, *refs), out_shape=(tile_type, sent(n_row, 2 * lines)), name="first"
+    )(part, moved, shares)
     first_got = swap(first_part, "row")
-    across_part = pl.pallas_call(across_kernel, out_shape=sent(n_col), name="across")(tile, first_got)
+    across_part = pl.pallas_call(
+        lambda *refs: across_kernel(wider, *refs), out_shape=sent(n_col), name="across"
+    )(tile, first_got)
     across_got = swap(across_part, "col")
     down_part = pl.pallas_call(down_kernel, out_shape=sent(n_row), name="down")(tile, across_got)
     down_got = swap(down_part, "row")
     balanced, row_bias, col_bias = pl.pallas_call(
-        lambda *refs: last_kernel(r_bins, *refs), out_shape=(tile_type, vec_type, vec_type), name="last"
+        lambda *refs: last_kernel(r_bins, wider, *refs),
+        out_shape=(tile_type, vec_type, vec_type),
+        name="last",
     )(tile, first_got, across_got, down_got)
     return (balanced, row_bias.reshape(-1), col_bias.reshape(-1))
 

time: 148 us -> 147 us (level)
  blocking collectives: 76.5 us -> 69 us
  Pallas kernels: 64 us -> 68.5 us
  starting transfers between devices: 3.41 us -> 6.96 us
  other arithmetic: 1.6 us -> 0 us
    all_to_all x1 -> x0, blocking collectives: 35.7 us -> none  [on_device(): lax.all_to_all(send, ('row', 'col'), split_axis=0, concat_axis=0, tiled=T...]
    all_to_all x4, blocking collectives: 40.8 us -> 69 us  [swap(): return lax.all_to_all(x, axis, split_axis=0, concat_axis=0, tiled=True)]
    pallas_call x5, Pallas kernels: 13.7 us -> 23.8 us  [the longest x1 11.2 us: row_share(): pl.pallas_call(lambda *refs: row_share_kernel(n_col, *refs), out_shape=ja...]
    all_to_all x0 -> x1, starting transfers between devices: none -> 3.54 us  [swap(): return lax.all_to_all(x, axis, split_axis=0, concat_axis=0, tiled=True)]
    pallas_call x1, Pallas kernels: 23.9 us -> 21.1 us  [bin_extra(): pl.pallas_call(extra_kernel, grid=(bin_steps,), out_shape=jax.ShapeDtypeS...]
    pallas_call x1, Pallas kernels: 24.2 us -> 21.5 us  [bin_main(): pl.pallas_call(main_kernel, grid=(bin_steps,), out_shape=jax.ShapeDtypeSt...]
    add x1 -> x0, other arithmetic: 1.6 us -> none  [on_device(): tile_id = (pair_rows[:, 0] >> 9) * n_col + (pair_cols[:, 0] >> 9)]
  transfers between devices with their start and end apart: 1 -> 2, of which waited for: 0 -> 0; matrix products, arithmetic and copies ran while one was open for 0% -> 0% of each run, Pallas kernels for 16% -> 22%
where the time goes in v2:
time: 147 us
  blocking collectives  69 us (47%)
  Pallas kernels  68.5 us (47%)
  starting transfers between devices  6.96 us (5%)
  local copies, waits for them, and re-layouts  1.66 us (1%)
    all_to_all x4, blocking collectives, swap(): return lax.all_to_all(x, axis, split_axis=0, concat_axis=0, tiled=True)  69 us
    pallas_call x1, Pallas kernels, bin_main(): pl.pallas_call(main_kernel, grid=(bin_steps,), out_shape=jax.ShapeDtypeSt...  21.5 us
    pallas_call x1, Pallas kernels, bin_extra(): pl.pallas_call(extra_kernel, grid=(bin_steps,), out_shape=jax.ShapeDtypeS...  21.1 us
    pallas_call x1, Pallas kernels, row_share(): pl.pallas_call(lambda *refs: row_share_kernel(n_col, *refs), out_shape=ja...  11.2 us
    pallas_call x1, Pallas kernels, pack(): pl.pallas_call(pack_kernel, out_shape=(jax.ShapeDtypeStruct((devices, 4 *...  5.12 us
    all_to_all x1, starting transfers between devices, swap(): return lax.all_to_all(x, axis, split_axis=0, concat_axis=0, tiled=True)  3.54 us
    ppermute x1, starting transfers between devices, on_device(): moved = lax.ppermute(extra, both, handed)  3.42 us
    pallas_call x1, Pallas kernels, on_device(): pl.pallas_call(lambda *refs: first_kernel(c_bins, *refs), out_shape=(tile...  2.97 us
  transfers between devices with their start and end apart: 2, of which 0 were waited for; matrix products, arithmetic and copies ran while one was open for 0% of the time, Pallas kernels for 22%

profile of v2, /device:TPU:1, one launch (start us, length us, event | category | flops | bytes accessed | tf_op | source)
XLA Modules:
  0.0 146.8 jit_solution(13970295402434447606)
XLA Ops:
  0.6 5.1 %pack.1 = (f32[128,24,128]{2,1,0:T(8,128)}, f32[144,768]{1,0:T(8,128)}) custom-call(s32[144]{0:T(256)} %counts_ref.1, s32[144,768]{1,0:T(8,128)} %refs_0_.1, s32[144,768]{1,0:T(8,128)} %cols_ref.1, f32[144,768]{1,0:T(8,128)} %wgt_ref.1), custom_call_target="tpu_custom_call" | custom-call | tf_op jit(solution)/shard_map/pack/pallas_call | solution.py:57
  5.7 35.7 %all_to_all.25.got_ref = f32[128,24,128]{2,1,0:T(8,128)} all-to-all(f32[128,24,128]{2,1,0:T(8,128)} %get-tuple-element.10), channel_id=1, replica_groups=mesh['row'=8,'col'=16] {'row','col'}, dimensions={0} | all-to-all | bytes 3145728 | tf_op jit(solution)/shard_map/all_to_all | solution.py:316
  41.4 21.1 %bin_extra.1.extra_ref = f32[512,512]{1,0:T(8,128)} custom-call(f32[128,24,128]{2,1,0:T(8,128)} %all_to_all.25.got_ref), custom_call_target="tpu_custom_call" | custom-call | flops 10000000000 | bytes 2000000 | tf_op jit(solution)/shard_map/bin_extra/pallas_call | solution.py:201
  62.6 3.4 %collective-permute-start = (f32[512,512]{1,0:T(8,128)}, f32[512,512]{1,0:T(8,128)S(1)}, u32[]{:S(2)}, u32[]{:S(2)}) collective-permute-start(f32[512,512]{1,0:T(8,128)} %bin_extra.1.extra_ref), channel_id=1, source_target_pairs={{16,0},{1,17},{50,34},{35,51},{84,68},{69,85},{118,102},{103,119}} | collective-permute-start | bytes 3145736 | tf_op jit(solution)/shard_map/ppermute | solution.py:324
  66.0 11.2 %row_share.1 = f32[128,4,128]{2,1,0:T(4,128)} custom-call(s32[144,768]{1,0:T(8,128)} %refs_0_.1, f32[144,768]{1,0:T(8,128)} %get-tuple-element.11.refs_1_), custom_call_target="tpu_custom_call" | custom-call | flops 1000000000 | bytes 1000000 | tf_op jit(solution)/shard_map/row_share/pallas_call | solution.py:98
  77.1 3.5 %all-to-all-start.1 = ((f32[128,4,128]{2,1,0:T(4,128)}), f32[128,4,128]{2,1,0:T(4,128)S(1)}, u32[]{:S(2)}, u32[]{:S(2)}) async-start(f32[128,4,128]{2,1,0:T(4,128)} %row_share.1), calls=%async_computation.1 | async-start | bytes 524288 | tf_op jit(solution)/shard_map/all_to_all | solution.py:316
  80.7 21.5 %bin_main.1.refs_0_ = f32[512,512]{1,0:T(8,128)} custom-call(f32[128,24,128]{2,1,0:T(8,128)} %all_to_all.25.got_ref, f32[512,512]{1,0:T(8,128)} %bin_extra.1.extra_ref), custom_call_target="tpu_custom_call" | custom-call | flops 10000000000 | bytes 2000000 | tf_op jit(solution)/shard_map/bin_main/pallas_call | solution.py:215
  102.2 0.0 all-to-all-done.1.refs_2_
  102.2 0.0 copy-start
  102.2 0.0 collective-permute-done.refs_1_
  102.2 0.7 copy-done
  102.9 0.0 copy-start.1
  102.9 1.0 copy-done.1
  103.8 3.0 %first.1 = (f32[512,512]{1,0:T(8,128)}, f32[8,8,128]{2,1,0:T(8,128)}) custom-call(f32[512,512]{1,0:T(8,128)} %bin_main.1.refs_0_, f32[512,512]{1,0:T(8,128)} %copy-done.1, f32[128,4,128]{2,1,0:T(4,128)} %copy-done), custom_call_target="tpu_custom_call" | custom-call | tf_op jit(solution)/shard_map/first/pallas_call | solution.py:327
  106.8 9.2 %all_to_all.26.refs_1_ = f32[8,8,128]{2,1,0:T(8,128)} all-to-all(f32[8,8,128]{2,1,0:T(8,128)} %get-tuple-element.13), channel_id=1, replica_groups=mesh['row'=8,'col'=16] {'row'}, dimensions={0} | all-to-all | bytes 65536 | tf_op jit(solution)/shard_map/all_to_all | solution.py:316
  116.0 2.0 %across.1 = f32[16,4,128]{2,1,0:T(4,128)} custom-call(f32[512,512]{1,0:T(8,128)} %get-tuple-element.12.refs_0_.tile_ref, f32[8,8,128]{2,1,0:T(8,128)} %all_to_all.26.refs_1_), custom_call_target="tpu_custom_call" | custom-call | tf_op jit(solution)/shard_map/across/pallas_call | solution.py:331
  118.0 13.4 %all_to_all.27.got_ref.refs_2_ = f32[16,4,128]{2,1,0:T(4,128)} all-to-all(f32[16,4,128]{2,1,0:T(4,128)} %across.1), channel_id=1, replica_groups=mesh['row'=8,'col'=16] {'col'}, dimensions={0} | all-to-all | bytes 65536 | tf_op jit(solution)/shard_map/all_to_all | solution.py:316
  131.4 2.1 %down.1 = f32[8,4,128]{2,1,0:T(4,128)} custom-call(f32[512,512]{1,0:T(8,128)} %get-tuple-element.12.refs_0_.tile_ref, f32[16,4,128]{2,1,0:T(4,128)} %all_to_all.27.got_ref.refs_2_), custom_call_target="tpu_custom_call" | custom-call | tf_op jit(solution)/shard_map/down/pallas_call | solution.py:335
  133.5 10.7 %all_to_all.28.refs_3_ = f32[8,4,128]{2,1,0:T(4,128)} all-to-all(f32[8,4,128]{2,1,0:T(4,128)} %down.1), channel_id=1, replica_groups=mesh['row'=8,'col'=16] {'row'}, dimensions={0} | all-to-all | bytes 32768 | tf_op jit(solution)/shard_map/all_to_all | solution.py:316
  144.2 2.6 %last.1 = (f32[512,512]{1,0:T(8,128)}, f32[4,128]{1,0:T(4,128)}, f32[4,128]{1,0:T(4,128)}) custom-call(f32[512,512]{1,0:T(8,128)} %get-tuple-element.12.refs_0_.tile_ref, f32[8,8,128]{2,1,0:T(8,128)} %all_to_all.26.refs_1_, f32[16,4,128]{2,1,0:T(4,128)} %all_to_all.27.got_ref.refs_2_, f32[8,4,128]{2,1,0:T(4,128)} %all_to_all.28.refs_3_), custom_call_target="tpu_custom_call" | custom-call | tf_op jit(solution)/shard_map/last/pallas_call | solution.py:337
Async XLA Ops:
  62.6 39.6 %collective-permute-start = (f32[512,512]{1,0:T(8,128)}, f32[512,512]{1,0:T(8,128)S(1)}, u32[]{:S(2)}, u32[]{:S(2)}) collective-permute-start(f32[512,512]{1,0:T(8,128)} %bin_extra.1.extra_ref), channel_id=1, source_target_pairs={{16,0},{1,17},{50,34},{35,51},{84,68},{69,85},{118,102},{103,119}} | collective-permute-start | bytes 3145736 | tf_op jit(solution)/shard_map/ppermute | solution.py:324
  77.1 25.0 %all-to-all-start.1 = ((f32[128,4,128]{2,1,0:T(4,128)}), f32[128,4,128]{2,1,0:T(4,128)S(1)}, u32[]{:S(2)}, u32[]{:S(2)}) async-start(f32[128,4,128]{2,1,0:T(4,128)} %row_share.1), calls=%async_computation.1 | async-start | bytes 524288 | tf_op jit(solution)/shard_map/all_to_all | solution.py:316
  102.2 0.7 copy-start
  102.9 1.0 copy-start.1
